TPU v7x, 32 devices: a whole 2x2x4 slice. The times are simulated.
32 devices in a mesh: dp: 8 (over z, y), mp: 4 (over x, core).
Axes of the slice: x: 2, y: 2, z: 4, core: 2. Of those that a mesh axis runs over, the one named last changes fastest.
Arguments:
- sentence_entry_words: bfloat16 [16384, 768], P(('dp', 'mp')), may hold values from -6 to 6
- sentence_present_marks: int32 [1024], P(('dp', 'mp')), may hold values 0 or 1
- picture_present_marks: int32 [1024], P(('dp', 'mp')), may hold values 0 or 1
- matched_picture_positions: int32 [1024], replicated, may hold values from 0 to 1023, each once
- stored_picture_patches: bfloat16 [51200, 768], P(('dp', 'mp')), may hold values from -6 to 6
- log_logit_multiplier: float32 [1], replicated, may hold values from 3.6 to 4.3
- leading_standardizer_stretch: float32 [768], replicated, may hold values from 0.5 to 1.5
- leading_standardizer_shift: float32 [768], replicated, may hold values from -1 to 1
- lookup_coefficients: bfloat16 [768, 768], P(None, 'mp'), may hold values from -0.21875 to 0.21875
- lookup_offset: float32 [768], P('mp'), may hold values from -1 to 1
- address_coefficients: bfloat16 [768, 768], P(None, 'mp'), may hold values from -0.21875 to 0.21875
- content_coefficients: bfloat16 [768, 768], P(None, 'mp'), may hold values from -0.21875 to 0.21875
- content_offset: float32 [768], P('mp'), may hold values from -1 to 1
- mixer_exit_coefficients: bfloat16 [768, 768], P('mp'), may hold values from -0.625 to 0.625
- mixer_exit_offset: float32 [768], replicated, may hold values from -1 to 1
- trailing_standardizer_stretch: float32 [768], replicated, may hold values from 0.5 to 1.5
- trailing_standardizer_shift: float32 [768], replicated, may hold values from -1 to 1
- perceptron_entry_coefficients: bfloat16 [768, 3072], P(None, 'mp'), may hold values from -0.21875 to 0.21875
- perceptron_inner_offset: float32 [3072], P('mp'), may hold values from -1 to 1
- perceptron_exit_coefficients: bfloat16 [3072, 768], P('mp'), may hold values from -0.109375 to 0.109375
- perceptron_exit_offset: float32 [768], replicated, may hold values from -1 to 1
- picture_lookup_coefficients: bfloat16 [768, 768], replicated, may hold values from -0.21875 to 0.21875
- picture_address_coefficients: bfloat16 [768, 768], replicated, may hold values from -0.21875 to 0.21875
- picture_content_coefficients: bfloat16 [768, 768], replicated, may hold values from -0.21875 to 0.21875
- picture_mixer_exit: bfloat16 [768, 768], replicated, may hold values from -0.625 to 0.625
- picture_perceptron_entry: bfloat16 [768, 3072], replicated, may hold values from -0.21875 to 0.21875
- picture_perceptron_exit: bfloat16 [3072, 768], replicated, may hold values from -0.109375 to 0.109375
Outputs:
- loss: float32 [1], replicated
- text_out: bfloat16 [16384, 768], P(('dp', 'mp'))
- text_in_grad: float32 [16384, 768], P(('dp', 'mp'))
- temperature_grad: float32 [1], replicated
- ln1_gain_grad: float32 [768], replicated
- ln1_bias_grad: float32 [768], replicated
- w_query_grad: float32 [768, 768], P(None, 'mp')
- query_bias_grad: float32 [768], P('mp')
- w_key_grad: float32 [768, 768], P(None, 'mp')
- w_value_grad: float32 [768, 768], P(None, 'mp')
- value_bias_grad: float32 [768], P('mp')
- w_attn_out_grad: float32 [768, 768], P('mp')
- attn_out_bias_grad: float32 [768], replicated
- ln2_gain_grad: float32 [768], replicated
- ln2_bias_grad: float32 [768], replicated
- w_hidden_grad: float32 [768, 3072], P(None, 'mp')
- hidden_bias_grad: float32 [3072], P('mp')
- w_proj_grad: float32 [3072, 768], P('mp')
- proj_bias_grad: float32 [768], replicated
Inputs may be any that keep to these rules, and one draw needn't show every extreme that they name: `matched_picture_positions`: each index appears exactly once.
All inputs are finite; a program needn't handle non-finite values. No bound on the sum of `sentence_present_marks` or of `picture_present_marks` on one device may be relied on, other than what follows from the above.
Results may differ from a plain program's by a relative error of at most 0.012.
Values may be sent and summed in bfloat16 or wider, within the bound.
A program may use at most 192 MiB of HBM per device.

v0:
```python
from functools import partial
import jax
import jax.numpy as jnp
from jax import lax
from jax.sharding import PartitionSpec as P

D = 768
HEADS = 12
HD = 64
LEN = 16
PATCHES = 50


def layer_norm(tensor, norm_gain, norm_shift):
    centred = tensor - jnp.mean(tensor, axis=-1, keepdims=True)
    variance = jnp.mean(centred * centred, axis=-1, keepdims=True)
    return centred * lax.rsqrt(variance + 1e-06) * norm_gain + norm_shift


def normalize(pooled):
    return pooled * lax.rsqrt(jnp.sum(pooled * pooled, axis=-1, keepdims=True) + 1e-06)


def product(left, right):
    return jnp.dot(left, right, preferred_element_type=jnp.float32)


def masked_scores(queries, key_rows, causal):
    scores = jnp.einsum(
        "gqhd,gkhd->ghqk", queries, key_rows, preferred_element_type=jnp.float32
    ) * HD ** (-0.5)
    if causal:
        places = jnp.arange(scores.shape[-1], dtype=jnp.int32)
        scores = jnp.where(places[None, :] <= places[:, None], scores, -1e30)
    return scores


def softmax_rows(scores):
    highest = jnp.max(scores, axis=-1, keepdims=True)
    weights = jnp.exp(scores - highest)
    totals = jnp.sum(weights, axis=-1, keepdims=True)
    return (weights / totals, highest + jnp.log(totals))


def attention_back(queries, key_rows, value_rows, log_totals, mixed_grad):
    scores = masked_scores(queries, key_rows, True)
    attn_probs = jnp.exp(scores - log_totals)
    probs_grad = jnp.einsum(
        "gqhd,gkhd->ghqk", mixed_grad, value_rows, preferred_element_type=jnp.float32
    )
    value_grad = jnp.einsum(
        "ghqk,gqhd->gkhd",
        attn_probs.astype(jnp.bfloat16),
        mixed_grad,
        preferred_element_type=jnp.float32,
    )
    inner_sum = jnp.sum(attn_probs * probs_grad, axis=-1, keepdims=True)
    score_grad = (attn_probs * (probs_grad - inner_sum)).astype(jnp.bfloat16)
    query_grad = jnp.einsum(
        "ghqk,gkhd->gqhd", score_grad, key_rows, preferred_element_type=jnp.float32
    ) * HD ** (-0.5)
    key_grad = jnp.einsum(
        "ghqk,gqhd->gkhd", score_grad, queries, preferred_element_type=jnp.float32
    ) * HD ** (-0.5)
    return (query_grad, key_grad, value_grad)


def image_embed(stored_picture_patches, frozen):
    (
        picture_lookup_coefficients,
        picture_address_coefficients,
        picture_content_coefficients,
        picture_mixer_exit,
        picture_perceptron_entry,
        picture_perceptron_exit,
    ) = frozen
    tokens = stored_picture_patches.astype(jnp.float32)
    examples = tokens.shape[0] // PATCHES
    normed = layer_norm(tokens, 1.0, 0.0).astype(jnp.bfloat16)
    grid_shape = (examples, PATCHES, HEADS, HD)
    queries = product(normed, picture_lookup_coefficients).astype(jnp.bfloat16).reshape(grid_shape)
    key_rows = (
        product(normed, picture_address_coefficients).astype(jnp.bfloat16).reshape(grid_shape)
    )
    value_rows = (
        product(normed, picture_content_coefficients).astype(jnp.bfloat16).reshape(grid_shape)
    )
    attn_probs, unused_totals = softmax_rows(masked_scores(queries, key_rows, False))
    mixed_heads = jnp.einsum(
        "ghqk,gkhd->gqhd",
        attn_probs.astype(jnp.bfloat16),
        value_rows,
        preferred_element_type=jnp.float32,
    )
    mixed_heads = mixed_heads.reshape(examples * PATCHES, D).astype(jnp.bfloat16)
    middle = tokens + product(mixed_heads, picture_mixer_exit)
    normed_two = layer_norm(middle, 1.0, 0.0).astype(jnp.bfloat16)
    hidden_act = jax.nn.gelu(
        product(normed_two, picture_perceptron_entry), approximate=True
    ).astype(jnp.bfloat16)
    output = middle + product(hidden_act, picture_perceptron_exit)
    return normalize(jnp.mean(output.reshape(examples, PATCHES, D), axis=1)).astype(jnp.bfloat16)


def embed(block_out):
    return normalize(jnp.mean(block_out.reshape(-1, LEN, D), axis=1))


def body(
    sentence_entry_words,
    sentence_present_marks,
    picture_present_marks,
    matched_picture_positions,
    stored_picture_patches,
    log_logit_multiplier,
    leading_standardizer_stretch,
    leading_standardizer_shift,
    lookup_coefficients,
    lookup_offset,
    address_coefficients,
    content_coefficients,
    content_offset,
    mixer_exit_coefficients,
    mixer_exit_offset,
    trailing_standardizer_stretch,
    trailing_standardizer_shift,
    perceptron_entry_coefficients,
    perceptron_inner_offset,
    perceptron_exit_coefficients,
    perceptron_exit_offset,
    picture_lookup_coefficients,
    picture_address_coefficients,
    picture_content_coefficients,
    picture_mixer_exit,
    picture_perceptron_entry,
    picture_perceptron_exit,
):
    own_count = sentence_present_marks.shape[0]
    mp_count = lax.axis_size("mp")
    rank = lax.axis_index("mp")
    text_mask, image_mask = (
        lax.all_gather(
            sentence_present_marks.astype(jnp.float32), ("dp", "mp"), axis=0, tiled=True
        ),
        lax.all_gather(picture_present_marks.astype(jnp.float32), ("dp", "mp"), axis=0, tiled=True),
    )
    wide = partial(lax.all_gather, axis_name="mp", axis=1, tiled=True)
    tall = partial(lax.all_gather, axis_name="mp", axis=0, tiled=True)
    w_q, w_k, w_v, w_o = (
        wide(lookup_coefficients),
        wide(address_coefficients),
        wide(content_coefficients),
        tall(mixer_exit_coefficients),
    )
    w_h, w_p = (wide(perceptron_entry_coefficients), tall(perceptron_exit_coefficients))
    b_q, b_v, b_h = (tall(lookup_offset), tall(content_offset), tall(perceptron_inner_offset))
    image_half = image_embed(
        stored_picture_patches,
        (
            picture_lookup_coefficients,
            picture_address_coefficients,
            picture_content_coefficients,
            picture_mixer_exit,
            picture_perceptron_entry,
            picture_perceptron_exit,
        ),
    )
    all_image = lax.all_gather(image_half, ("dp", "mp"), axis=0, tiled=True)
    tokens = sentence_entry_words.astype(jnp.float32)
    all_rows = tokens.shape[0]
    normed_one, norm_one_back = jax.vjp(
        layer_norm, tokens, leading_standardizer_stretch, leading_standardizer_shift
    )
    normed_one = normed_one.astype(jnp.bfloat16)
    grid_shape = (all_rows // LEN, LEN, HEADS, HD)
    queries = (product(normed_one, w_q) + b_q).astype(jnp.bfloat16).reshape(grid_shape)
    key_rows = product(normed_one, w_k).astype(jnp.bfloat16).reshape(grid_shape)
    value_rows = (product(normed_one, w_v) + b_v).astype(jnp.bfloat16).reshape(grid_shape)
    attn_probs, log_totals = softmax_rows(masked_scores(queries, key_rows, True))
    mixed_heads = jnp.einsum(
        "ghqk,gkhd->gqhd",
        attn_probs.astype(jnp.bfloat16),
        value_rows,
        preferred_element_type=jnp.float32,
    )
    mixed_heads = mixed_heads.reshape(all_rows, D).astype(jnp.bfloat16)
    middle = tokens + product(mixed_heads, w_o) + mixer_exit_offset
    normed_two, norm_two_back = jax.vjp(
        layer_norm, middle, trailing_standardizer_stretch, trailing_standardizer_shift
    )
    normed_two = normed_two.astype(jnp.bfloat16)
    hidden_pre = product(normed_two, w_h) + b_h
    hidden_act, gelu_back = jax.vjp(partial(jax.nn.gelu, approximate=True), hidden_pre)
    hidden_act = hidden_act.astype(jnp.bfloat16)
    output = middle + product(hidden_act, w_p) + perceptron_exit_offset
    text_emb, embed_back = jax.vjp(embed, output)
    text_half = text_emb.astype(jnp.bfloat16)
    everyone = text_mask.shape[0]
    order = jnp.arange(everyone, dtype=jnp.int32)
    offset = lax.axis_index(("dp", "mp")) * own_count
    own_pair = lax.dynamic_slice_in_dim(matched_picture_positions, offset, own_count, 0)
    own_text = sentence_present_marks.astype(jnp.float32)
    hits = (order[None, :] == own_pair[:, None]).astype(jnp.float32)
    text_weight = own_text * jnp.sum(hits * image_mask[None, :], axis=1)
    inverse = jnp.zeros((everyone,), jnp.int32).at[matched_picture_positions].set(order)
    image_weight = image_mask * text_mask[inverse]
    logit_multiplier = jnp.exp(log_logit_multiplier[0])
    logits = logit_multiplier * jnp.einsum(
        "id,jd->ij", text_half, all_image, preferred_element_type=jnp.float32
    )
    weights = jnp.exp(logits)
    row_weights = weights * image_mask[None, :]
    row_total = jnp.sum(row_weights, axis=1)
    column_weights = weights * own_text[:, None]
    column_total = lax.psum(jnp.sum(column_weights, axis=0), ("dp", "mp"))
    pair_total = jnp.sum(image_weight)
    safe_row = jnp.where(row_total > 0, row_total, 1.0)
    safe_column = jnp.where(column_total > 0, column_total, 1.0)
    hit_logit = jnp.sum(hits * logits, axis=1)
    column_part = 0.5 * jnp.sum(image_weight * jnp.log(safe_column))
    total_part = 0.5 * jnp.sum(text_weight * jnp.log(safe_row)) - jnp.sum(text_weight * hit_logit)
    row_grad = 0.5 * text_weight[:, None] * (row_weights / safe_row[:, None] - hits)
    column_grad = 0.5 * image_weight[None, :] * (column_weights / safe_column[None, :] - hits)
    temp_part = jnp.sum((row_grad + column_grad) * logits)
    text_grad = product((logit_multiplier * row_grad).astype(jnp.bfloat16), all_image) + product(
        (logit_multiplier * column_grad).astype(jnp.bfloat16), all_image
    )
    token_grad = embed_back(text_grad)[0]
    proj_bias_grad = jnp.sum(token_grad, axis=0)
    grad_rows = token_grad.astype(jnp.bfloat16)
    w_proj_grad = jnp.einsum("rf,rd->fd", hidden_act, grad_rows, preferred_element_type=jnp.float32)
    active_grad = jnp.einsum("rd,fd->rf", grad_rows, w_p, preferred_element_type=jnp.float32)
    hidden_grad = gelu_back(active_grad)[0].astype(jnp.bfloat16)
    w_hidden_grad = jnp.einsum(
        "rd,rf->df", normed_two, hidden_grad, preferred_element_type=jnp.float32
    )
    hidden_bias_grad = jnp.sum(hidden_grad.astype(jnp.float32), axis=0)
    normed_two_grad = jnp.einsum("rf,df->rd", hidden_grad, w_h, preferred_element_type=jnp.float32)
    norm_two_grads = norm_two_back(normed_two_grad)
    middle_grad = token_grad + norm_two_grads[0]
    attn_bias_grad = jnp.sum(middle_grad, axis=0)
    attn_grad_rows = middle_grad.astype(jnp.bfloat16)
    w_attn_out_grad = jnp.einsum(
        "rk,rd->kd", mixed_heads, attn_grad_rows, preferred_element_type=jnp.float32
    )
    mixed_grad = jnp.einsum("rd,kd->rk", attn_grad_rows, w_o, preferred_element_type=jnp.float32)
    mixed_grad = mixed_grad.astype(jnp.bfloat16).reshape(grid_shape)
    query_grad, key_grad, value_grad = attention_back(
        queries, key_rows, value_rows, log_totals, mixed_grad
    )
    query_grad = query_grad.reshape(all_rows, D).astype(jnp.bfloat16)
    key_grad = key_grad.reshape(all_rows, D).astype(jnp.bfloat16)
    value_grad = value_grad.reshape(all_rows, D).astype(jnp.bfloat16)
    back = partial(jnp.einsum, "rd,rk->dk", normed_one, preferred_element_type=jnp.float32)
    w_query_grad, w_key_grad, w_value_grad = (back(query_grad), back(key_grad), back(value_grad))
    query_bias_grad = jnp.sum(query_grad.astype(jnp.float32), axis=0)
    value_bias_grad = jnp.sum(value_grad.astype(jnp.float32), axis=0)
    down = partial(jnp.einsum, "rk,dk->rd", preferred_element_type=jnp.float32)
    normed_one_grad = down(query_grad, w_q) + down(key_grad, w_k) + down(value_grad, w_v)
    norm_one_grads = norm_one_back(normed_one_grad)
    text_in_grad = middle_grad + norm_one_grads[0]

    def share(grad, axis):
        part = lax.psum_scatter(grad.astype(jnp.bfloat16), "mp", scatter_dimension=axis, tiled=True)
        return lax.psum(part, "dp").astype(jnp.float32)

    shared = lax.psum(
        (
            total_part,
            temp_part,
            norm_one_grads[1],
            norm_one_grads[2],
            attn_bias_grad,
            norm_two_grads[1],
            norm_two_grads[2],
            proj_bias_grad,
            query_bias_grad,
            value_bias_grad,
            hidden_bias_grad,
        ),
        ("dp", "mp"),
    )
    loss = jnp.reshape((shared[0] + column_part) / pair_total, (1,))

    def own(vector):
        return lax.dynamic_slice_in_dim(
            vector, rank * (vector.shape[0] // mp_count), vector.shape[0] // mp_count, 0
        )

    return (
        loss,
        output.astype(jnp.bfloat16),
        text_in_grad,
        jnp.reshape(shared[1], (1,)),
        shared[2],
        shared[3],
        share(w_query_grad, 1),
        own(shared[8]),
        share(w_key_grad, 1),
        share(w_value_grad, 1),
        own(shared[9]),
        share(w_attn_out_grad, 0),
        shared[4],
        shared[5],
        shared[6],
        share(w_hidden_grad, 1),
        own(shared[10]),
        share(w_proj_grad, 0),
        shared[7],
    )


def solution(mesh):
    in_specs = (
        P(("dp", "mp"), None),
        P(("dp", "mp")),
        P(("dp", "mp")),
        P(),
        P(("dp", "mp"), None),
        P(),
        P(),
        P(),
        P(None, "mp"),
        P("mp"),
        P(None, "mp"),
        P(None, "mp"),
        P("mp"),
        P("mp", None),
        P(),
        P(),
        P(),
        P(None, "mp"),
        P("mp"),
        P("mp", None),
        P(),
        P(),
        P(),
        P(),
        P(),
        P(),
        P(),
    )
    out_specs = (
        P(),
        P(("dp", "mp"), None),
        P(("dp", "mp"), None),
        P(),
        P(),
        P(),
        P(None, "mp"),
        P("mp"),
        P(None, "mp"),
        P(None, "mp"),
        P("mp"),
        P("mp", None),
        P(),
        P(),
        P(),
        P(None, "mp"),
        P("mp"),
        P("mp", None),
        P(),
    )
    return jax.shard_map(body, mesh=mesh, in_specs=in_specs, out_specs=out_specs, check_vma=False)
```

profile of v0, /device:TPU:0, one launch (start us, length us, event | category | flops | bytes accessed | tf_op | source)
XLA Modules:
  0.0 737.5 jit_solution(3353801001150994818)
XLA Ops:
  18.3 8.5 %reshape.272 = bf16[32,50,12,64]{3,2,1,0:T(8,128)(2,1)} reshape(bf16[1600,768]{1,0:T(8,128)(2,1)} %convolution_convert_fusion.2) | data formatting | bytes 4915200 | tf_op jit(solution)/shard_map/reshape | solution.py:83
  26.8 5.4 convolution_convert_fusion.3
  32.2 8.6 %reshape.271 = bf16[32,50,12,64]{3,2,1,0:T(8,128)(2,1)} reshape(bf16[1600,768]{1,0:T(8,128)(2,1)} %convolution_convert_fusion.3) | data formatting | bytes 4915200 | tf_op jit(solution)/shard_map/reshape | solution.py:81
  40.8 11.8 %fusion.26 = f32[32,12,50,50]{2,3,1,0:T(8,128)} fusion(bf16[32,50,12,64]{3,2,1,0:T(8,128)(2,1)} %reshape.272, bf16[32,50,12,64]{3,2,1,0:T(8,128)(2,1)} %reshape.271), kind=kOutput, calls=%fused_computation.35 | convolution fusion | flops 122880000 | bytes 8755200 | tf_op jit(solution)/shard_map/gqhd,gkhd->ghqk/dot_general | solution.py:29
  52.7 15.2 %fusion.112 = (f32[32,12,50]{2,1,0:T(8,128)S(1)}, f32[32,12,50,50]{2,3,1,0:T(8,128)}) fusion(f32[32,12,50,50]{2,3,1,0:T(8,128)} %fusion.26), kind=kOutput, calls=%fused_computation.197 | output fusion | flops 3840049 | bytes 7756800 | tf_op jit(solution)/shard_map/sub | solution.py:40
  71.5 8.5 %reshape.270 = bf16[32,50,12,64]{3,2,1,0:T(8,128)(2,1)} reshape(bf16[1600,768]{1,0:T(8,128)(2,1)} %convolution_convert_fusion.4) | data formatting | bytes 4915200 | tf_op jit(solution)/shard_map/reshape | solution.py:86
  80.0 9.3 %convert_bitcast_fusion = bf16[32,50,12,64]{3,1,2,0:T(8,128)(2,1)} fusion(f32[32,12,50,50]{2,3,1,0:T(8,128)} %get-tuple-element.69, f32[32,12,50]{2,1,0:T(8,128)S(1)} %get-tuple-element.68, bf16[32,50,12,64]{3,2,1,0:T(8,128)(2,1)} %reshape.270), kind=kOutput, calls=%fused_computation.39 | convolution fusion | flops 126028800 | bytes 8832000 | tf_op jit(solution)/shard_map/ghqk,gkhd->gqhd/dot_general | solution.py:89
  89.3 9.6 %copy.116 = bf16[32,50,12,64]{1,0,3,2:T(8,128)(2,1)} copy(bf16[32,50,12,64]{3,1,2,0:T(8,128)(2,1)} %convert_bitcast_fusion) | data formatting | bytes 4915200 | tf_op jit(solution)/shard_map/convert_element_type | solution.py:95
  98.9 11.7 %convert_element_type.211 = bf16[1600,768]{0,1:T(8,128)(2,1)} reshape(bf16[32,50,12,64]{1,0,3,2:T(8,128)(2,1)} %copy.116) | data formatting | bytes 4915200 | tf_op jit(solution)/shard_map/convert_element_type | solution.py:95
  110.7 4.8 fusion.113
  117.7 23.4 %fusion.34 = f32[1600,768]{1,0:T(8,128)} fusion(f32[1600,768]{1,0:T(8,128)} %copy-done.14, bf16[3072,768]{1,0:T(8,128)(2,1)} %param.53, bf16[768,3072]{1,0:T(8,128)(2,1)} %param.52, f32[1600]{0:T(1024)S(1)} %add_rsqrt_fusion, f32[1600]{0:T(1024)S(1)} %broadcast_multiply_fusion), kind=kOutput, calls=%fused_computation.48 | convolution fusion | flops 15148646400 | bytes 19280384 | tf_op jit(solution)/shard_map/dot_general | solution.py:25
  141.1 5.4 reshape.231
  151.5 42.6 %all-reduce = f32[1024]{0:T(1024)S(1)} all-reduce(f32[1024]{0:T(1024)S(1)} %convert_dynamic-update-slice_fusion), channel_id=1, replica_groups=mesh['dp'=8,'mp'=4] {'dp','mp'}, use_global_device_ids=true, to_apply=%add | all-reduce | flops 1024 | bytes 8192
  195.9 5.5 all-gather
  202.2 4.3 scatter_custom_fusion
  208.2 8.0 %all-reduce.6 = (f32[768]{0:T(1024)S(1)}, f32[768]{0:T(1024)S(1)}) all-reduce(f32[768]{0:T(1024)S(1)} %dynamic-update-slice.2, f32[768]{0:T(1024)S(1)} %dynamic-update-slice.1), channel_id=1, replica_groups=mesh['dp'=8,'mp'=4] {'mp'}, use_global_device_ids=true, to_apply=%add.2 | all-reduce | flops 1536 | bytes 12288
  237.9 4.1 convert_element_type.199
  246.8 8.2 %fusion.99 = f32[512,3072]{1,0:T(8,128)} fusion(bf16[768,3072]{1,0:T(8,128)(2,1)} %all-gather.17.cloned.1.call-done, f32[512,768]{1,0:T(8,128)} %copy-done.11, f32[768]{0:T(1024)S(1)} %copy-done.85, f32[768]{0:T(1024)S(1)} %copy-done.65, f32[512]{0:T(512)S(1)} %fusion.92, f32[512]{0:T(512)S(1)} %broadcast_multiply_fusion.3), kind=kOutput, calls=%fused_computation.194 | convolution fusion | flops 2417885184 | bytes 12593152 | tf_op jit(solution)/shard_map/dot_general | solution.py:25
  255.1 9.6 %bitcast_reduce_fusion = (f32[32,768]{1,0:T(8,128)S(1)}, bf16[512,768]{1,0:T(8,128)(2,1)}) fusion(f32[768]{0:T(1024)S(1)} %copy-done.82, f32[512,768]{1,0:T(8,128)} %copy-done.11, bf16[3072,768]{1,0:T(8,128)(2,1)} %all-gather.19.cloned.1.call-done, f32[512,3072]{1,0:T(8,128)} %fusion.99, f32[3072]{0:T(1024)S(1)} %bitcast.68), kind=kOutput, calls=%fused_computation.87 | convolution fusion | flops 2433196032 | bytes 13483008 | tf_op jit(solution)/shard_map/dot_general | solution.py:25
  271.1 39.8 %all-reduce.5 = (f32[1024]{0:T(1024)}, f32[1024]{0:T(1024)S(1)}) all-reduce(f32[1024]{0:T(1024)} %get-tuple-element.28, f32[1024]{0:T(1024)} %copy-done.47), channel_id=1, replica_groups=mesh['dp'=8,'mp'=4] {'dp','mp'}, use_global_device_ids=true, to_apply=%region_24.25 | all-reduce | flops 2048 | bytes 16384 | tf_op jit(solution)/shard_map/psum | solution.py:215
  310.8 9.0 %gather_fusion = f32[1024]{0:T(1024)} fusion(f32[1024]{0:T(1024)S(1)} %get-tuple-element.47, s32[1024]{0:T(1024)} %fusion.88), kind=kCustom, calls=%fused_computation | custom fusion | bytes 12288 | tf_op jit(solution)/shard_map/gather | solution.py:206
  325.0 10.2 %convert_reduce_fusion.1 = (f32[3072]{0:T(1024)}, bf16[512,3072]{1,0:T(8,128)(2,1)S(1)}) fusion(f32[512,3072]{1,0:T(8,128)} %fusion.99, f32[3072]{0:T(1024)S(1)} %bitcast.69, bf16[512,768]{1,0:T(8,128)(2,1)S(1)} %bitcast_convert_fusion, bf16[3072,768]{1,0:T(8,128)(2,1)} %all-gather.19.cloned.1.call-done), kind=kOutput, calls=%fused_computation.30 | convolution fusion | flops 2452091904 | bytes 14966784 | tf_op jit(solution)/shard_map/rd,fd->rf/dot_general | solution.py:232
  368.3 3.9 convert_element_type.229
  387.6 6.5 convolution_convert_fusion.1
  395.3 8.8 %convolution_convert_fusion = bf16[3072,768]{1,0:T(8,128)(2,1)} fusion(bf16[512,768]{1,0:T(8,128)(2,1)S(1)} %copy-done.29, f32[512,3072]{1,0:T(8,128)} %fusion.99, f32[3072]{0:T(1024)S(1)} %bitcast.70), kind=kOutput, calls=%fused_computation.42 | convolution fusion | flops 2434007040 | bytes 11808768 | tf_op jit(solution)/shard_map/rf,rd->fd/dot_general | solution.py:231
  404.2 13.8 %reduce-scatter.9.cloned.1.call-done = bf16[768,192]{0,1:T(8,128)(2,1)} async-done(((bf16[768,768]{0,1:T(8,128)(2,1)}), bf16[768,192]{0,1:T(8,128)(2,1)}) %reduce-scatter.9.cloned.1.call-update) | async-done | bytes 294928 | tf_op jit(solution)/shard_map/reduce_scatter | solution.py:264
  418.0 28.6 %reduce-scatter.11.cloned.1.call-done = bf16[768,192]{0,1:T(8,128)(2,1)} async-done(((bf16[768,768]{0,1:T(8,128)(2,1)}), bf16[768,192]{0,1:T(8,128)(2,1)}) %reduce-scatter.11.cloned.1.call-update) | async-done | bytes 294928 | tf_op jit(solution)/shard_map/reduce_scatter | solution.py:264
  446.6 28.2 %reduce-scatter.13.cloned.1.call-done = bf16[192,768]{1,0:T(8,128)(2,1)} async-done(((bf16[768,768]{1,0:T(8,128)(2,1)}), bf16[192,768]{1,0:T(8,128)(2,1)}) %reduce-scatter.13.cloned.1.call-update) | async-done | bytes 294928 | tf_op jit(solution)/shard_map/reduce_scatter | solution.py:264
  474.9 50.3 %reduce-scatter.15.cloned.1.call-done = bf16[768,768]{1,0:T(8,128)(2,1)} async-done(((bf16[768,3072]{1,0:T(8,128)(2,1)}), bf16[768,768]{1,0:T(8,128)(2,1)}) %reduce-scatter.15.cloned.1.call-update) | async-done | bytes 1179664 | tf_op jit(solution)/shard_map/reduce_scatter | solution.py:264
  525.1 50.5 %reduce-scatter.17.cloned.1.call-done = bf16[768,768]{1,0:T(8,128)(2,1)} async-done(((bf16[3072,768]{1,0:T(8,128)(2,1)}), bf16[768,768]{1,0:T(8,128)(2,1)}) %reduce-scatter.17.cloned.1.call-update) | async-done | bytes 1179664 | tf_op jit(solution)/shard_map/reduce_scatter | solution.py:264
  587.8 45.1 %all-reduce.4 = (f32[]{:T(128)}, f32[1]{0:T(128)}, f32[768]{0:T(1024)}, f32[768]{0:T(1024)}, f32[768]{0:T(1024)S(1)}, /*index=5*/f32[768]{0:T(1024)S(1)}, f32[76...) all-reduce(f32[]{:T(128)S(6)} %sub.88, ...), channel_id=1, replica_groups=mesh['dp'=8,'mp'=4] {'dp','mp'}, use_global_device_ids=true, to_apply=%region_21.22 | all-reduce | flops 9218 | bytes 73744 | tf_op jit(solution)/shard_map/psum | solution.py:267
  636.9 83.1 %all-reduce.10.cloned.1.call-done = (bf16[768,192]{0,1:T(8,128)(2,1)}, bf16[768,192]{0,1:T(8,128)(2,1)}, bf16[768,192]{0,1:T(8,128)(2,1)}, bf16[192,768]{1,0:T(8...) async-done(((bf16[768,192]{0,1:T(8,128)(2,1)}, bf16[768,192]{0,1:T(8,128)(2,1)}, bf16[768,192]{0,1:T(8,128)(2,1)}, bf16[192,768]{1,0:T(8,128)(2,1)}, ...) | async-done | bytes 3538960 | tf_op jit(solution)/shard_map/psum | solution.py:265
  (321 shorter events, 133.8 us)
Async XLA Ops:
  7.2 103.5 %copy-start = (bf16[768,768]{1,0:T(8,128)(2,1)S(1)}, bf16[768,768]{1,0:T(8,128)(2,1)}, u32[]{:S(2)}) copy-start(bf16[768,768]{1,0:T(8,128)(2,1)} %param.51) | copy-start | bytes 3538948
  7.2 209.1 %all-gather.13.cloned.1.call-start = ((), (), s32[]{:S(2)}) async-start(), calls=%async_computation.8 | async-start | bytes 1474560 | tf_op jit(solution)/shard_map/all_gather | solution.py:151
  7.9 212.8 %all-gather.11.cloned.1.call-start = ((), (), s32[]{:S(2)}) async-start(), calls=%async_computation.7 | async-start | bytes 1474560 | tf_op jit(solution)/shard_map/all_gather | solution.py:150
  8.7 216.5 %all-gather.9.cloned.1.call-start = ((), (), s32[]{:S(2)}) async-start(), calls=%async_computation.6 | async-start | bytes 1474560 | tf_op jit(solution)/shard_map/all_gather | solution.py:152
  9.4 232.6 %all-gather.15.cloned.1.call-start = ((), (), s32[]{:S(2)}) async-start(), calls=%async_computation.9 | async-start | bytes 1474560 | tf_op jit(solution)/shard_map/all_gather | solution.py:153
  10.0 236.8 %all-gather.17.cloned.1.call-start = ((), (), s32[]{:S(2)}) async-start(), calls=%async_computation.10 | async-start | bytes 5898240 | tf_op jit(solution)/shard_map/all_gather | solution.py:155
  10.6 244.4 %all-gather.19.cloned.1.call-start = ((), (), s32[]{:S(2)}) async-start(), calls=%async_computation.11 | async-start | bytes 5898240 | tf_op jit(solution)/shard_map/all_gather | solution.py:155
  11.2 254.8 %all-gather.21.cloned.1.call-start = ((), (), s32[]{:S(2)}) async-start(), calls=%async_computation.12 | async-start | bytes 1622016 | tf_op jit(solution)/shard_map/all_gather | solution.py:168
  52.7 15.2 %copy-start.8 = (bf16[1600,768]{1,0:T(8,128)(2,1)S(1)}, bf16[1600,768]{1,0:T(8,128)(2,1)}, u32[]{:S(2)}) copy-start(bf16[1600,768]{1,0:T(8,128)(2,1)} %param.31) | copy-start | bytes 7372804
  52.7 15.2 %copy-start.79 = (bf16[768,768]{1,0:T(8,128)(2,1)S(1)}, bf16[768,768]{1,0:T(8,128)(2,1)}, u32[]{:S(2)}) copy-start(bf16[768,768]{1,0:T(8,128)(2,1)} %param.50) | copy-start | bytes 3538948
  146.5 47.7 %copy-start.64 = (s32[1024]{0:T(1024)S(1)}, s32[1024]{0:T(1024)}, u32[]{:S(2)}) copy-start(s32[1024]{0:T(1024)} %param.30) | copy-start | bytes 12292
  146.5 48.3 %copy-start.2 = (bf16[512,768]{1,0:T(8,128)(2,1)S(1)}, bf16[512,768]{1,0:T(8,128)(2,1)}, u32[]{:S(2)}) copy-start(bf16[512,768]{1,0:T(8,128)(2,1)} %param.27) | copy-start | bytes 2359300
  146.5 48.8 %copy-start.88 = (u32[32]{0:T(128)S(1)}, u32[32]{0:T(128)}, u32[]{:S(2)}) copy-start(u32[32]{0:T(128)} %constant.94) | copy-start | bytes 388
  146.5 49.4 %copy-start.63 = (f32[768]{0:T(1024)S(1)}, f32[768]{0:T(1024)}, u32[]{:S(2)}) copy-start(f32[768]{0:T(1024)} %param.45) | copy-start | bytes 9220
  146.5 61.2 %copy-start.72 = (f32[192]{0:T(256)S(1)}, f32[192]{0:T(256)}, u32[]{:S(2)}) copy-start(f32[192]{0:T(256)} %param.36) | copy-start | bytes 2308
  146.5 61.5 %copy-start.73 = (f32[192]{0:T(256)S(1)}, f32[192]{0:T(256)}, u32[]{:S(2)}) copy-start(f32[192]{0:T(256)} %param.39) | copy-start | bytes 2308
  146.6 69.7 %copy-start.34 = (f32[768]{0:T(1024)S(1)}, f32[768]{0:T(1024)}, u32[]{:S(2)}) copy-start(f32[768]{0:T(1024)} %param.33) | copy-start | bytes 9220
  146.6 69.7 %copy-start.83 = (f32[768]{0:T(1024)S(1)}, f32[768]{0:T(1024)}, u32[]{:S(2)}) copy-start(f32[768]{0:T(1024)} %param.34) | copy-start | bytes 9220
  150.7 253.6 %reduce-scatter.7.cloned.1.call-start = ((), (), s32[]{:S(2)}) async-start(), calls=%async_computation.13 | async-start | bytes 1474560 | tf_op jit(solution)/shard_map/reduce_scatter | solution.py:264
  195.3 21.0 %copy-start.43 = (f32[512]{0:T(512)}, f32[512]{0:T(512)S(1)}, u32[]{:S(2)}) copy-start(f32[512]{0:T(512)S(1)} %fusion.54) | copy-start | bytes 6148
  195.3 29.9 %copy-start.39 = (f32[512]{0:T(512)}, f32[512]{0:T(512)S(1)}, u32[]{:S(2)}) copy-start(f32[512]{0:T(512)S(1)} %fusion.91) | copy-start | bytes 6148
  201.4 53.6 %copy-start.49 = (f32[4,1,768]{2,1,0:T(1,128)}, f32[4,1,768]{2,1,0:T(1,128)S(1)}, u32[]{:S(2)}) copy-start(f32[4,1,768]{2,1,0:T(1,128)S(1)} %all-gather) | copy-start | bytes 36868
  255.1 11.0 %copy-start.55 = (s32[32]{0:T(128)S(1)}, s32[32]{0:T(128)}, u32[]{:S(2)}) copy-start(s32[32]{0:T(128)} %dynamic_slice.12) | copy-start | bytes 388
  268.7 54.5 %copy-start.17 = (f32[32,1024]{1,0:T(8,128)}, f32[32,1024]{1,0:T(8,128)S(1)}, u32[]{:S(2)}) copy-start(f32[32,1024]{1,0:T(8,128)S(1)} %get-tuple-element.78) | copy-start | bytes 393220
  363.3 54.7 %reduce-scatter.9.cloned.1.call-start = ((), (), s32[]{:S(2)}) async-start(), calls=%async_computation.14 | async-start | bytes 1474560 | tf_op jit(solution)/shard_map/reduce_scatter | solution.py:264
  375.6 71.0 %reduce-scatter.11.cloned.1.call-start = ((), (), s32[]{:S(2)}) async-start(), calls=%async_computation.15 | async-start | bytes 1474560 | tf_op jit(solution)/shard_map/reduce_scatter | solution.py:264
  384.4 90.5 %reduce-scatter.13.cloned.1.call-start = ((), (), s32[]{:S(2)}) async-start(), calls=%async_computation.16 | async-start | bytes 1474560 | tf_op jit(solution)/shard_map/reduce_scatter | solution.py:264
  387.5 137.6 %reduce-scatter.15.cloned.1.call-start = ((), (), s32[]{:S(2)}) async-start(), calls=%async_computation.17 | async-start | bytes 5898240 | tf_op jit(solution)/shard_map/reduce_scatter | solution.py:264
  394.2 181.5 %reduce-scatter.17.cloned.1.call-start = ((), (), s32[]{:S(2)}) async-start(), calls=%async_computation.18 | async-start | bytes 5898240 | tf_op jit(solution)/shard_map/reduce_scatter | solution.py:264
  404.1 171.6 %copy-start.54 = (f32[12,64]{1,0:T(8,128)S(1)}, f32[12,64]{1,0:T(8,128)}, u32[]{:S(2)}) copy-start(f32[12,64]{1,0:T(8,128)} %get-tuple-element.85) | copy-start | bytes 9220
  404.1 171.7 %copy-start.31 = (bf16[512,768]{1,0:T(8,128)(2,1)S(1)}, bf16[512,768]{1,0:T(8,128)(2,1)}, u32[]{:S(2)}) copy-start(bf16[512,768]{1,0:T(8,128)(2,1)} %convert_element_type.226) | copy-start | bytes 2359300
  404.1 315.9 %all-reduce.10.cloned.1.call-start = ((), (), s32[]{:S(2)}) async-start(), calls=%async_computation.19 | async-start | bytes 7077888 | tf_op jit(solution)/shard_map/psum | solution.py:265
  (74 other events, 281.9 us)
Sparse Core Ops, SparseCore 0:
  9.6 20.1 all-gather.12
  31.3 17.4 all-gather.10
  50.4 17.4 all-gather.8
  69.2 17.4 all-gather.14
  88.1 37.4 all-gather.16
  127.0 37.9 all-gather.18
  168.4 55.1 all-gather.20
  363.4 25.7 reduce-scatter.6
  392.3 25.6 reduce-scatter.8
  421.0 25.6 reduce-scatter.10
  449.2 25.6 reduce-scatter.12
  477.2 47.8 reduce-scatter.14
  527.6 47.9 reduce-scatter.16
  579.8 140.1 all-reduce.9
where the time goes:
time: 745 us; the launch traced here: 737 us
  waiting for transfers between devices  258 us (35%)
  matrix products  160 us (21%)
  blocking collectives  141 us (19%)
  local copies, waits for them, and re-layouts  110 us (15%)
  other arithmetic  46 us (6%)
  between operations  21.1 us (3%)
    reduce_scatter x6, waiting for transfers between devices, share(): lax.psum_scatter(grad.astype(jnp.bfloat16), 'mp', scatter_dimension=axis,...  171 us
    psum x1, waiting for transfers between devices, share(): return lax.psum(part, 'dp').astype(jnp.float32)  83.1 us
    dot_general x13, matrix products, product(): return jnp.dot(left, right, preferred_element_type=jnp.float32)  71.3 us
    unnamed x2, blocking collectives  50.7 us
    psum x1, blocking collectives, body(): lax.psum((total_part, temp_part, norm_one_grads[1], norm_one_grads[2], at...  45.1 us
    psum x1, blocking collectives, body(): column_total = lax.psum(jnp.sum(column_weights, axis=0), ('dp', 'mp'))  39.8 us
    convert_element_type x2, local copies, waits for them, and re-layouts, image_embed(): mixed_heads.reshape(examples * PATCHES, D).astype(jnp.bfloat16)  21.4 us
    dot_general x2, matrix products, masked_scores(): jnp.einsum('gqhd,gkhd->ghqk', queries, key_rows, preferred_element_type=j...  15.3 us
  transfers between devices with their start and end apart: 14, of which 6 were waited for; matrix products, arithmetic and copies ran while one was open for 33% of the time, Pallas kernels for 0%

commit v1 on v0

--- a/solution.py
+++ b/solution.py
@@ -262,7 +262,7 @@
 
     def share(grad, axis):
         part = lax.psum_scatter(grad.astype(jnp.bfloat16), "mp", scatter_dimension=axis, tiled=True)
-        return lax.psum(part, "dp").astype(jnp.float32)
+        return jnp.sum(lax.all_gather(part, "dp"), axis=0).astype(jnp.float32)
 
     shared = lax.psum(
         (

time: 745 us -> 1090 us (1.46)
  waiting for transfers between devices: 258 us -> 579 us
  other arithmetic: 46 us -> 61.8 us
    all_gather x0 -> x6, waiting for transfers between devices: none -> 404 us  [share(): return jnp.sum(lax.all_gather(part, 'dp'), axis=0).astype(jnp.float32)]
    psum x1 -> x0, waiting for transfers between devices: 83.1 us -> none  [share(): return lax.psum(part, 'dp').astype(jnp.float32)]
    reduce_sum x0 -> x6, other arithmetic: none -> 18.8 us  [share(): return jnp.sum(lax.all_gather(part, 'dp'), axis=0).astype(jnp.float32)]
  transfers between devices with their start and end apart: 14 -> 19, of which waited for: 6 -> 10; matrix products, arithmetic and copies ran while one was open for 33% -> 25% of each run, Pallas kernels for 0% -> 0%
where the time goes in v1:
time: 1090 us; the launch traced here: 1080 us
  waiting for transfers between devices  579 us (53%)
  matrix products  160 us (15%)
  blocking collectives  138 us (13%)
  local copies, waits for them, and re-layouts  117 us (11%)
  other arithmetic  61.8 us (6%)
  between operations  21.3 us (2%)
    all_gather x6, waiting for transfers between devices, share(): return jnp.sum(lax.all_gather(part, 'dp'), axis=0).astype(jnp.float32)  404 us
    reduce_scatter x6, waiting for transfers between devices, share(): lax.psum_scatter(grad.astype(jnp.bfloat16), 'mp', scatter_dimension=axis,...  170 us
    dot_general x13, matrix products, product(): return jnp.dot(left, right, preferred_element_type=jnp.float32)  71.3 us
    unnamed x2, blocking collectives  50.2 us
    psum x1, blocking collectives, body(): lax.psum((total_part, temp_part, norm_one_grads[1], norm_one_grads[2], at...  42.1 us
    psum x1, blocking collectives, body(): column_total = lax.psum(jnp.sum(column_weights, axis=0), ('dp', 'mp'))  40.1 us
  transfers between devices with their start and end apart: 19, of which 10 were waited for; matrix products, arithmetic and copies ran while one was open for 25% of the time, Pallas kernels for 0%

profile of v1, /device:TPU:0, one launch (start us, length us, event | category | flops | bytes accessed | tf_op | source)
XLA Modules:
  0.0 1078.8 jit_solution(8029125271282272563)
XLA Ops:
  18.3 8.6 reshape.278
  32.2 8.7 reshape.277
  40.9 12.2 %fusion.26 = f32[32,12,50,50]{2,3,1,0:T(8,128)} fusion(bf16[32,50,12,64]{3,2,1,0:T(8,128)(2,1)} %reshape.278, bf16[32,50,12,64]{3,2,1,0:T(8,128)(2,1)} %reshape.277), kind=kOutput, calls=%fused_computation.35 | convolution fusion | flops 122880000 | bytes 8755200 | tf_op jit(solution)/shard_map/gqhd,gkhd->ghqk/dot_general | solution.py:29
  53.1 15.2 %fusion.112 = (f32[32,12,50]{2,1,0:T(8,128)S(1)}, f32[32,12,50,50]{2,3,1,0:T(8,128)}) fusion(f32[32,12,50,50]{2,3,1,0:T(8,128)} %fusion.26), kind=kOutput, calls=%fused_computation.200 | output fusion | flops 3840049 | bytes 7756800 | tf_op jit(solution)/shard_map/sub | solution.py:40
  71.9 8.5 reshape.276
  80.4 9.3 convert_bitcast_fusion
  89.8 9.8 copy.116
  99.5 11.8 %convert_element_type.223 = bf16[1600,768]{0,1:T(8,128)(2,1)} reshape(bf16[32,50,12,64]{1,0,3,2:T(8,128)(2,1)} %copy.116) | data formatting | bytes 4915200 | tf_op jit(solution)/shard_map/convert_element_type | solution.py:95
  118.3 23.4 %fusion.34 = f32[1600,768]{1,0:T(8,128)} fusion(f32[1600,768]{1,0:T(8,128)} %copy-done.14, bf16[3072,768]{1,0:T(8,128)(2,1)} %param.53, bf16[768,3072]{1,0:T(8,128)(2,1)} %param.52, f32[1600]{0:T(1024)S(1)} %add_rsqrt_fusion, f32[1600]{0:T(1024)S(1)} %broadcast_multiply_fusion), kind=kOutput, calls=%fused_computation.48 | convolution fusion | flops 15148646400 | bytes 19280384 | tf_op jit(solution)/shard_map/dot_general | solution.py:25
  152.2 42.2 %all-reduce = f32[1024]{0:T(1024)S(1)} all-reduce(f32[1024]{0:T(1024)S(1)} %convert_dynamic-update-slice_fusion), channel_id=1, replica_groups=mesh['dp'=8,'mp'=4] {'dp','mp'}, use_global_device_ids=true, to_apply=%add | all-reduce | flops 1024 | bytes 8192
  196.1 5.5 all-gather.6
  208.4 8.0 all-reduce.6
  247.0 8.2 fusion.99
  255.2 9.6 bitcast_reduce_fusion.3
  271.2 40.1 %all-reduce.5 = (f32[1024]{0:T(1024)}, f32[1024]{0:T(1024)S(1)}) all-reduce(f32[1024]{0:T(1024)} %get-tuple-element.28, f32[1024]{0:T(1024)} %copy-done.44), channel_id=1, replica_groups=mesh['dp'=8,'mp'=4] {'dp','mp'}, use_global_device_ids=true, to_apply=%region_24.25 | all-reduce | flops 2048 | bytes 16384 | tf_op jit(solution)/shard_map/psum | solution.py:215
  311.3 9.0 gather_fusion
  325.4 10.2 convert_reduce_fusion.1
  388.2 6.5 convolution_convert_fusion.1
  395.9 8.9 convolution_convert_fusion
  405.4 13.0 %reduce-scatter.9.cloned.1.call-done = bf16[768,192]{0,1:T(8,128)(2,1)} async-done(((bf16[768,768]{0,1:T(8,128)(2,1)}), bf16[768,192]{0,1:T(8,128)(2,1)}) %reduce-scatter.9.cloned.1.call-update) | async-done | bytes 294928 | tf_op jit(solution)/shard_map/reduce_scatter | solution.py:264
  418.5 28.6 %reduce-scatter.11.cloned.1.call-done = bf16[768,192]{0,1:T(8,128)(2,1)} async-done(((bf16[768,768]{0,1:T(8,128)(2,1)}), bf16[768,192]{0,1:T(8,128)(2,1)}) %reduce-scatter.11.cloned.1.call-update) | async-done | bytes 294928 | tf_op jit(solution)/shard_map/reduce_scatter | solution.py:264
  447.2 28.2 %reduce-scatter.13.cloned.1.call-done = bf16[192,768]{1,0:T(8,128)(2,1)} async-done(((bf16[768,768]{1,0:T(8,128)(2,1)}), bf16[192,768]{1,0:T(8,128)(2,1)}) %reduce-scatter.13.cloned.1.call-update) | async-done | bytes 294928 | tf_op jit(solution)/shard_map/reduce_scatter | solution.py:264
  475.4 50.2 %reduce-scatter.15.cloned.1.call-done = bf16[768,768]{1,0:T(8,128)(2,1)} async-done(((bf16[768,3072]{1,0:T(8,128)(2,1)}), bf16[768,768]{1,0:T(8,128)(2,1)}) %reduce-scatter.15.cloned.1.call-update) | async-done | bytes 1179664 | tf_op jit(solution)/shard_map/reduce_scatter | solution.py:264
  525.6 50.4 %reduce-scatter.17.cloned.1.call-done = bf16[768,768]{1,0:T(8,128)(2,1)} async-done(((bf16[3072,768]{1,0:T(8,128)(2,1)}), bf16[768,768]{1,0:T(8,128)(2,1)}) %reduce-scatter.17.cloned.1.call-update) | async-done | bytes 1179664 | tf_op jit(solution)/shard_map/reduce_scatter | solution.py:264
  588.2 42.1 %all-reduce.4 = (f32[]{:T(128)}, f32[1]{0:T(128)}, f32[768]{0:T(1024)}, f32[768]{0:T(1024)}, f32[768]{0:T(1024)S(1)}, /*index=5*/f32[768]{0:T(1024)S(1)}, f32[76...) all-reduce(f32[]{:T(128)S(6)} %sub.88, ...), channel_id=1, replica_groups=mesh['dp'=8,'mp'=4] {'dp','mp'}, use_global_device_ids=true, to_apply=%region_21.22 | all-reduce | flops 9218 | bytes 73744 | tf_op jit(solution)/shard_map/psum | solution.py:267
  639.0 44.0 %all-gather.37.cloned.1.call-done = bf16[6144,192]{0,1:T(8,128)(2,1)} async-done(((bf16[768,192]{0,1:T(8,128)(2,1)}), bf16[6144,192]{0,1:T(8,128)(2,1)}) %all-gather.37.cloned.1.call-update) | async-done | bytes 2359312 | tf_op jit(solution)/shard_map/all_gather | solution.py:265
  687.9 47.7 %all-gather.39.cloned.1.call-done = bf16[6144,192]{0,1:T(8,128)(2,1)} async-done(((bf16[768,192]{0,1:T(8,128)(2,1)}), bf16[6144,192]{0,1:T(8,128)(2,1)}) %all-gather.39.cloned.1.call-update) | async-done | bytes 2359312 | tf_op jit(solution)/shard_map/all_gather | solution.py:265
  740.5 47.4 %all-gather.41.cloned.1.call-done = bf16[1536,768]{1,0:T(8,128)(2,1)} async-done(((bf16[192,768]{1,0:T(8,128)(2,1)}), bf16[1536,768]{1,0:T(8,128)(2,1)}) %all-gather.41.cloned.1.call-update) | async-done | bytes 2359312 | tf_op jit(solution)/shard_map/all_gather | solution.py:265
  790.8 134.9 %all-gather.43.cloned.1.call-done = bf16[6144,768]{1,0:T(8,128)(2,1)} async-done(((bf16[768,768]{1,0:T(8,128)(2,1)}), bf16[6144,768]{1,0:T(8,128)(2,1)}) %all-gather.43.cloned.1.call-update) | async-done | bytes 9437200 | tf_op jit(solution)/shard_map/all_gather | solution.py:265
  925.7 5.7 reduce_sum.496
  933.0 130.3 %all-gather.45.cloned.1.call-done = bf16[6144,768]{1,0:T(8,128)(2,1)} async-done(((bf16[768,768]{1,0:T(8,128)(2,1)}), bf16[6144,768]{1,0:T(8,128)(2,1)}) %all-gather.45.cloned.1.call-update) | async-done | bytes 9437200 | tf_op jit(solution)/shard_map/all_gather | solution.py:265
  1063.3 5.8 reduce_sum.498
  (339 shorter events, 173.6 us)
Async XLA Ops:
  7.2 104.2 %copy-start = (bf16[768,768]{1,0:T(8,128)(2,1)S(1)}, bf16[768,768]{1,0:T(8,128)(2,1)}, u32[]{:S(2)}) copy-start(bf16[768,768]{1,0:T(8,128)(2,1)} %param.51) | copy-start | bytes 3538948
  7.2 209.3 %all-gather.25.cloned.1.call-start = ((), (), s32[]{:S(2)}) async-start(), calls=%async_computation.8 | async-start | bytes 1474560 | tf_op jit(solution)/shard_map/all_gather | solution.py:151
  7.9 213.0 %all-gather.23.cloned.1.call-start = ((), (), s32[]{:S(2)}) async-start(), calls=%async_computation.7 | async-start | bytes 1474560 | tf_op jit(solution)/shard_map/all_gather | solution.py:150
  8.7 216.7 %all-gather.21.cloned.1.call-start = ((), (), s32[]{:S(2)}) async-start(), calls=%async_computation.6 | async-start | bytes 1474560 | tf_op jit(solution)/shard_map/all_gather | solution.py:152
  9.4 232.7 %all-gather.27.cloned.1.call-start = ((), (), s32[]{:S(2)}) async-start(), calls=%async_computation.9 | async-start | bytes 1474560 | tf_op jit(solution)/shard_map/all_gather | solution.py:153
  10.0 237.0 %all-gather.29.cloned.1.call-start = ((), (), s32[]{:S(2)}) async-start(), calls=%async_computation.10 | async-start | bytes 5898240 | tf_op jit(solution)/shard_map/all_gather | solution.py:155
  10.6 244.6 %all-gather.31.cloned.1.call-start = ((), (), s32[]{:S(2)}) async-start(), calls=%async_computation.11 | async-start | bytes 5898240 | tf_op jit(solution)/shard_map/all_gather | solution.py:155
  11.2 255.0 %all-gather.33.cloned.1.call-start = ((), (), s32[]{:S(2)}) async-start(), calls=%async_computation.12 | async-start | bytes 1622016 | tf_op jit(solution)/shard_map/all_gather | solution.py:168
  147.2 47.2 %copy-start.61 = (s32[1024]{0:T(1024)S(1)}, s32[1024]{0:T(1024)}, u32[]{:S(2)}) copy-start(s32[1024]{0:T(1024)} %param.30) | copy-start | bytes 12292
  147.2 47.8 %copy-start.2 = (bf16[512,768]{1,0:T(8,128)(2,1)S(1)}, bf16[512,768]{1,0:T(8,128)(2,1)}, u32[]{:S(2)}) copy-start(bf16[512,768]{1,0:T(8,128)(2,1)} %param.27) | copy-start | bytes 2359300
  147.2 48.3 %copy-start.85 = (u32[32]{0:T(128)S(1)}, u32[32]{0:T(128)}, u32[]{:S(2)}) copy-start(u32[32]{0:T(128)} %constant.101) | copy-start | bytes 388
  147.2 48.9 %copy-start.60 = (f32[768]{0:T(1024)S(1)}, f32[768]{0:T(1024)}, u32[]{:S(2)}) copy-start(f32[768]{0:T(1024)} %param.45) | copy-start | bytes 9220
  147.2 60.7 %copy-start.69 = (f32[192]{0:T(256)S(1)}, f32[192]{0:T(256)}, u32[]{:S(2)}) copy-start(f32[192]{0:T(256)} %param.36) | copy-start | bytes 2308
  147.2 61.0 %copy-start.70 = (f32[192]{0:T(256)S(1)}, f32[192]{0:T(256)}, u32[]{:S(2)}) copy-start(f32[192]{0:T(256)} %param.39) | copy-start | bytes 2308
  147.2 69.3 %copy-start.31 = (f32[768]{0:T(1024)S(1)}, f32[768]{0:T(1024)}, u32[]{:S(2)}) copy-start(f32[768]{0:T(1024)} %param.33) | copy-start | bytes 9220
  147.2 69.3 %copy-start.80 = (f32[768]{0:T(1024)S(1)}, f32[768]{0:T(1024)}, u32[]{:S(2)}) copy-start(f32[768]{0:T(1024)} %param.34) | copy-start | bytes 9220
  151.3 253.5 %reduce-scatter.7.cloned.1.call-start = ((), (), s32[]{:S(2)}) async-start(), calls=%async_computation.13 | async-start | bytes 1474560 | tf_op jit(solution)/shard_map/reduce_scatter | solution.py:264
  201.7 53.6 %copy-start.46 = (f32[4,1,768]{2,1,0:T(1,128)}, f32[4,1,768]{2,1,0:T(1,128)S(1)}, u32[]{:S(2)}) copy-start(f32[4,1,768]{2,1,0:T(1,128)S(1)} %all-gather.6) | copy-start | bytes 36868
  268.9 54.8 %copy-start.17 = (f32[32,1024]{1,0:T(8,128)}, f32[32,1024]{1,0:T(8,128)S(1)}, u32[]{:S(2)}) copy-start(f32[32,1024]{1,0:T(8,128)S(1)} %get-tuple-element.72) | copy-start | bytes 393220
  363.9 54.6 %reduce-scatter.9.cloned.1.call-start = ((), (), s32[]{:S(2)}) async-start(), calls=%async_computation.14 | async-start | bytes 1474560 | tf_op jit(solution)/shard_map/reduce_scatter | solution.py:264
  376.2 70.9 %reduce-scatter.11.cloned.1.call-start = ((), (), s32[]{:S(2)}) async-start(), calls=%async_computation.15 | async-start | bytes 1474560 | tf_op jit(solution)/shard_map/reduce_scatter | solution.py:264
  385.0 90.4 %reduce-scatter.13.cloned.1.call-start = ((), (), s32[]{:S(2)}) async-start(), calls=%async_computation.16 | async-start | bytes 1474560 | tf_op jit(solution)/shard_map/reduce_scatter | solution.py:264
  388.1 137.4 %reduce-scatter.15.cloned.1.call-start = ((), (), s32[]{:S(2)}) async-start(), calls=%async_computation.17 | async-start | bytes 5898240 | tf_op jit(solution)/shard_map/reduce_scatter | solution.py:264
  394.8 181.3 %reduce-scatter.17.cloned.1.call-start = ((), (), s32[]{:S(2)}) async-start(), calls=%async_computation.18 | async-start | bytes 5898240 | tf_op jit(solution)/shard_map/reduce_scatter | solution.py:264
  404.8 171.3 %copy-start.51 = (f32[12,64]{1,0:T(8,128)S(1)}, f32[12,64]{1,0:T(8,128)}, u32[]{:S(2)}) copy-start(f32[12,64]{1,0:T(8,128)} %get-tuple-element.79) | copy-start | bytes 9220
  404.8 171.4 %copy-start.28 = (bf16[512,768]{1,0:T(8,128)(2,1)S(1)}, bf16[512,768]{1,0:T(8,128)(2,1)}, u32[]{:S(2)}) copy-start(bf16[512,768]{1,0:T(8,128)(2,1)} %convert_element_type.238) | copy-start | bytes 2359300
  404.8 229.3 %all-gather.35.cloned.1.call-start = ((), (), s32[]{:S(2)}) async-start(), calls=%async_computation.19 | async-start | bytes 2654208 | tf_op jit(solution)/shard_map/all_gather | solution.py:265
  405.4 277.6 %all-gather.37.cloned.1.call-start = ((), (), s32[]{:S(2)}) async-start(), calls=%async_computation.20 | async-start | bytes 2654208 | tf_op jit(solution)/shard_map/all_gather | solution.py:265
  418.5 317.1 %all-gather.39.cloned.1.call-start = ((), (), s32[]{:S(2)}) async-start(), calls=%async_computation.21 | async-start | bytes 2654208 | tf_op jit(solution)/shard_map/all_gather | solution.py:265
  447.1 340.7 %all-gather.41.cloned.1.call-start = ((), (), s32[]{:S(2)}) async-start(), calls=%async_computation.22 | async-start | bytes 2654208 | tf_op jit(solution)/shard_map/all_gather | solution.py:265
  475.3 450.4 %all-gather.43.cloned.1.call-start = ((), (), s32[]{:S(2)}) async-start(), calls=%async_computation.23 | async-start | bytes 10616832 | tf_op jit(solution)/shard_map/all_gather | solution.py:265
  525.6 537.8 %all-gather.45.cloned.1.call-start = ((), (), s32[]{:S(2)}) async-start(), calls=%async_computation.24 | async-start | bytes 10616832 | tf_op jit(solution)/shard_map/all_gather | solution.py:265
  (76 other events, 364.0 us)
Sparse Core Ops, SparseCore 0:
  9.6 20.1 all-gather.24
  31.3 17.4 all-gather.22
  50.4 17.4 all-gather.20
  69.2 17.4 all-gather.26
  88.1 37.4 all-gather.28
  127.0 37.7 all-gather.30
  168.3 55.2 all-gather.32
  364.0 25.6 reduce-scatter.6
  392.8 25.6 reduce-scatter.8
  421.4 25.6 reduce-scatter.10
  449.7 25.6 reduce-scatter.12
  477.7 47.7 reduce-scatter.14
  528.1 47.9 reduce-scatter.16
  578.1 52.2 all-gather.34
  632.4 50.5 all-gather.36
  685.0 50.5 all-gather.38
  737.6 50.1 all-gather.40
  789.9 135.7 all-gather.42
  927.9 135.4 all-gather.44
